TPU v7x, 128 devices: a whole 4x4x4 slice. The times are simulated.
128 devices in a mesh: row: 8 (over y, core), col: 16 (over z, x).
Axes of the slice: x: 4, y: 4, z: 4, core: 2. Of those that a mesh axis runs over, the one named last changes fastest.
Arguments:
- b_three: bfloat16 [256, 384, 1536], P(('row', 'col')), may hold values from -0.47851562 to 0.47851562
- e_occ: float32 [256], replicated, may hold values from -1.5 to -0.3
- e_vir: float32 [384], replicated, may hold values from 0.2 to 3
- c_occ: bfloat16 [768, 256], replicated, may hold values from -0.375 to 0.375
- pair_list: int32 [128, 16, 2], P(('row', 'col')), may hold values from 0 to 255, as said below
- pair_live: int32 [128, 16], P(('row', 'col')), may hold values from 0 to 1, as said below
Outputs:
- gamma_ao: bfloat16 [384, 1536, 768], P('row', 'col')
Inputs may be any that keep to these rules, and one draw needn't show every extreme that they name: pair_list[w, p, 0] is one of the orbitals 2 w to 2 w + 1; pair_list[w, p, 1] is one of the orbitals 2 q to 2 q + 1 with q = (w // 16) * 16 + p. `pair_live`: every worker lists between 1 and 16 pairs; some worker lists all 16.
All inputs are finite; a program needn't handle non-finite values.
Results may differ from a plain program's by a relative error of at most 0.0053.
Values may be sent and summed in bfloat16 or wider, within the bound.
No kernel may reach another device: no remote copies, remote signals or barrier semaphores. Data moves between devices by JAX's collectives and lax.ppermute only.
A program may use at most 128 MiB of HBM per device.

v0:
```python
import jax
import jax.numpy as jnp
from jax import lax
from jax.sharding import PartitionSpec as P


def local(b_three, e_occ, e_vir, c_occ, pair_list, pair_live):
    own_count = b_three.shape[0]
    virt_count = b_three.shape[1]
    aux_count = b_three.shape[2]
    peer_count = lax.axis_size("col")
    row_count = lax.axis_size("row")

    def pair_step(gamma, peer, right_slab):
        first_orb = pair_list[0, peer, 0]
        second_orb = pair_list[0, peer, 1]
        listed_flag = pair_live[0, peer]
        own_slot = first_orb % own_count
        left_slab = lax.dynamic_index_in_dim(b_three, own_slot, 0, keepdims=False)
        integrals = lax.dot_general(
            left_slab, right_slab, (((1,), (1,)), ((), ())), preferred_element_type=jnp.float32
        )
        denominator = e_occ[first_orb] + e_occ[second_orb] - e_vir[:, None] - e_vir[None, :]
        amplitude = integrals / denominator
        weighted = (2.0 * amplitude - amplitude.T).astype(jnp.bfloat16)
        addition = jnp.dot(weighted, right_slab, preferred_element_type=jnp.float32)
        current = lax.dynamic_index_in_dim(gamma, own_slot, 0, keepdims=False)
        return lax.dynamic_update_index_in_dim(
            gamma, current + listed_flag.astype(jnp.float32) * addition, own_slot, 0
        )

    gamma = jnp.zeros(b_three.shape, jnp.float32)

    def fold_peers(gamma, piece):
        count = piece.shape[0] // own_count

        def visit(position, gamma):
            wanted = pair_list[0, position, 1] % own_count
            right_slab = lax.dynamic_index_in_dim(
                piece, position * own_count + wanted, 0, keepdims=False
            )
            return pair_step(gamma, position, right_slab)

        return lax.fori_loop(0, count, visit, gamma)

    gamma = fold_peers(gamma, lax.all_gather(b_three, "col", axis=0, tiled=True))
    gamma_mo = gamma.astype(jnp.bfloat16)
    virt_local = virt_count // row_count
    aux_local = aux_count // peer_count
    total_orbs = c_occ.shape[1]
    blocks = gamma_mo.reshape(own_count, row_count, virt_local, peer_count, aux_local)
    blocks = jnp.transpose(blocks, (1, 3, 0, 2, 4)).reshape(
        row_count * peer_count, own_count, virt_local * aux_local
    )
    regrouped = lax.all_to_all(blocks, ("row", "col"), split_axis=0, concat_axis=0, tiled=True)
    moved = regrouped.reshape(total_orbs, virt_local * aux_local)
    result = lax.dot_general(
        moved, c_occ, (((0,), (1,)), ((), ())), preferred_element_type=jnp.float32
    ).astype(jnp.bfloat16)
    return result.reshape(virt_local, aux_local, c_occ.shape[0])


def solution(mesh):
    return jax.shard_map(
        local,
        mesh=mesh,
        in_specs=(
            P(("row", "col"), None, None),
            P(),
            P(),
            P(),
            P(("row", "col"), None, None),
            P(("row", "col"), None),
        ),
        out_specs=P("row", "col", None),
        check_vma=False,
    )
```

profile of v0, /device:TPU:1, one launch (start us, length us, event | category | flops | bytes accessed | tf_op | source)
XLA Modules:
  0.0 638.8 jit_solution(17668714508559472050)
XLA Ops:
  7.3 223.8 %all-gather.2.cloned.1.call-done = bf16[32,384,1536]{2,1,0:T(8,128)(2,1)} async-done(((bf16[2,384,1536]{2,1,0:T(8,128)(2,1)}), bf16[32,384,1536]{2,1,0:T(8,128)(2,1)}) %all-gather.2.cloned.1.call-update) | async-done | bytes 37748752 | tf_op jit(solution)/shard_map/all_gather | solution.py:46
  233.9 331.1 %while.15 = (s32[]{:T(128)}, f32[2,384,1536]{2,1,0:T(8,128)}, s32[1,16,2]{1,2,0:T(2,128)S(1)}, s32[1,16]{1,0:T(1,128)S(1)}, bf16[2,384,1536]{2,1,0:T(8,128)(2,1)...) while((s32[]{:T(128)}, f32[2,384,1536]{2,1,0:T(8,128)}, ...), condition=%wide.region_1.2_spmd, body=%wide.region_0.1_spmd.sunk | while | flops 908181888 | bytes 53686384 | solution.py:44
  249.5 2.9 fusion.40
  270.2 2.9 fusion.40
  290.9 2.9 fusion.40
  311.6 2.9 fusion.40
  332.2 2.9 fusion.40
  352.9 2.9 fusion.40
  373.6 2.9 fusion.40
  394.3 2.9 fusion.40
  415.0 2.9 fusion.40
  435.7 2.9 fusion.40
  456.4 2.9 fusion.40
  477.1 2.9 fusion.40
  497.8 2.9 fusion.40
  518.5 2.9 fusion.40
  539.2 2.9 fusion.40
  559.8 2.9 fusion.40
  564.9 4.0 convert_element_type.29
  569.0 4.9 reshape.22
  576.4 5.1 reshape.23
  583.9 40.1 %all_to_all.5 = bf16[128,2,4608]{2,1,0:T(2,128)(2,1)} all-to-all(bf16[128,2,4608]{2,1,0:T(2,128)(2,1)S(1)} %copy.15), channel_id=1, replica_groups=mesh['row'=8,'col'=16] {'row','col'}, dimensions={0} | all-to-all | bytes 4718592 | tf_op jit(solution)/shard_map/all_to_all | solution.py:55
  624.0 2.9 reshape.24
  626.9 5.0 convolution_convert_fusion
  (191 shorter events, 166.0 us)
Async XLA Ops:
  6.5 620.4 %copy-start = (bf16[768,256]{1,0:T(8,128)(2,1)S(1)}, bf16[768,256]{1,0:T(8,128)(2,1)}, u32[]{:S(2)}) copy-start(bf16[768,256]{1,0:T(8,128)(2,1)} %param.11) | copy-start | bytes 1179652
  6.5 224.6 %all-gather.2.cloned.1.call-start = ((), (), s32[]{:S(2)}) async-start(), calls=%async_computation.1 | async-start | bytes 40108032 | tf_op jit(solution)/shard_map/all_gather | solution.py:46
  7.3 226.6 %copy-start.3 = (f32[384]{0:T(512)S(1)}, f32[384]{0:T(512)}, u32[]{:S(2)}) copy-start(f32[384]{0:T(512)} %param.10) | copy-start | bytes 4612
  7.3 226.6 %copy-start.4 = (f32[256]{0:T(256)S(1)}, f32[256]{0:T(256)}, u32[]{:S(2)}) copy-start(f32[256]{0:T(256)} %param.9) | copy-start | bytes 3076
  7.3 226.6 %copy-start.5 = (s32[1,16,2]{1,2,0:T(2,128)S(1)}, s32[1,16,2]{1,2,0:T(2,128)}, u32[]{:S(2)}) copy-start(s32[1,16,2]{1,2,0:T(2,128)} %param.12) | copy-start | bytes 388
  7.3 226.6 %copy-start.6 = (s32[1,16]{1,0:T(1,128)S(1)}, s32[1,16]{1,0:T(1,128)}, u32[]{:S(2)}) copy-start(s32[1,16]{1,0:T(1,128)} %param.13) | copy-start | bytes 196
  246.4 3.1 copy-start.1
  252.4 2.2 copy-start.2
  267.1 3.1 copy-start.1
  287.8 3.1 copy-start.1
  308.5 3.1 copy-start.1
  314.5 2.2 copy-start.2
  329.2 3.1 copy-start.1
  349.9 3.1 copy-start.1
  370.6 3.1 copy-start.1
  391.3 3.1 copy-start.1
  412.0 3.1 copy-start.1
  432.6 3.1 copy-start.1
  453.3 3.1 copy-start.1
  474.0 3.1 copy-start.1
  494.7 3.1 copy-start.1
  515.4 3.1 copy-start.1
  536.1 3.1 copy-start.1
  556.8 3.1 copy-start.1
  (14 other events, 30.6 us)
Sparse Core Ops, SparseCore 0:
  9.5 221.5 all-gather.1
where the time goes:
time: 642 us; the launch traced here: 639 us
  waiting for transfers between devices  225 us (35%)
  local copies, waits for them, and re-layouts  129 us (20%)
  loops' own time  127 us (20%)
  matrix products  90.1 us (14%)
  blocking collectives  40.1 us (6%)
  other arithmetic  14.6 us (2%)
  between operations  13.5 us (2%)
    all_gather x1, waiting for transfers between devices, local(): lax.all_gather(b_three, 'col', axis=0, tiled=True)  224 us
    another operation x1, loops' own time, fold_peers(): return lax.fori_loop(0, count, visit, gamma)  127 us
    while x64, local copies, waits for them, and re-layouts  52 us
    dot_general x16, matrix products, pair_step(): addition = jnp.dot(weighted, right_slab, preferred_element_type=jnp.float32)  46.4 us
    all_to_all x1, blocking collectives, local(): lax.all_to_all(blocks, ('row', 'col'), split_axis=0, concat_axis=0, tiled...  40.1 us
    dot_general x16, matrix products, pair_step(): lax.dot_general(left_slab, right_slab, (((1,), (1,)), ((), ())), preferre...  38.7 us
    dynamic_slice x16, local copies, waits for them, and re-layouts, pair_step(): current = lax.dynamic_index_in_dim(gamma, own_slot, 0, keepdims=False)  31.6 us
  transfers between devices with their start and end apart: 1, of which 1 were waited for; matrix products, arithmetic and copies ran while one was open for 0% of the time, Pallas kernels for 0%

commit v1 on v0

--- a/solution.py
+++ b/solution.py
@@ -2,6 +2,13 @@
 import jax.numpy as jnp
 from jax import lax
 from jax.sharding import PartitionSpec as P
+
+
+def gather_over(array, axis, dim):
+    size = lax.axis_size(axis)
+    pieces = jnp.stack([array for _ in range(size)])
+    pieces = lax.all_to_all(pieces, axis, split_axis=0, concat_axis=0)
+    return jnp.concatenate(pieces, axis=dim)
 
 
 def local(b_three, e_occ, e_vir, c_occ, pair_list, pair_live):
@@ -43,7 +50,7 @@
 
         return lax.fori_loop(0, count, visit, gamma)
 
-    gamma = fold_peers(gamma, lax.all_gather(b_three, "col", axis=0, tiled=True))
+    gamma = fold_peers(gamma, gather_over(b_three, "col", 0))
     gamma_mo = gamma.astype(jnp.bfloat16)
     virt_local = virt_count // row_count
     aux_local = aux_count // peer_count

time: 642 us -> 956 us (1.49)
  waiting for transfers between devices: 225 us -> 564 us
  local copies, waits for them, and re-layouts: 129 us -> 99.2 us
  matrix products: 90.1 us -> 115 us
  loops' own time: 127 us -> 113 us
  between operations: 13.5 us -> 0.06 us
    all_to_all x0 -> x1, waiting for transfers between devices: none -> 564 us  [gather_over(): pieces = lax.all_to_all(pieces, axis, split_axis=0, concat_axis=0)]
    all_gather x1 -> x0, waiting for transfers between devices: 224 us -> none  [local(): lax.all_gather(b_three, 'col', axis=0, tiled=True)]
    while x64 -> x0, local copies, waits for them, and re-layouts: 52 us -> none
    dot_general x16, matrix products: 46.4 us -> 71 us  [pair_step(): addition = jnp.dot(weighted, right_slab, preferred_element_type=jnp.float32)]
    another operation x1, loops' own time: 127 us -> 113 us  [fold_peers(): return lax.fori_loop(0, count, visit, gamma)]
    another operation x0 -> x1, local copies, waits for them, and re-layouts: none -> 13.6 us  [gather_over(): pieces = jnp.stack([array for _ in range(size)])]
    dot_general x16, local copies, waits for them, and re-layouts: 3.68 us -> 16.9 us  [pair_step(): lax.dot_general(left_slab, right_slab, (((1,), (1,)), ((), ())), preferre...]
where the time goes in v1:
time: 956 us; the launch traced here: 952 us
  waiting for transfers between devices  564 us (59%)
  matrix products  115 us (12%)
  loops' own time  113 us (12%)
  local copies, waits for them, and re-layouts  99.2 us (10%)
  blocking collectives  38.8 us (4%)
  other arithmetic  13.7 us (1%)
    all_to_all x1, waiting for transfers between devices, gather_over(): pieces = lax.all_to_all(pieces, axis, split_axis=0, concat_axis=0)  564 us
    another operation x1, loops' own time, fold_peers(): return lax.fori_loop(0, count, visit, gamma)  113 us
    dot_general x16, matrix products, pair_step(): addition = jnp.dot(weighted, right_slab, preferred_element_type=jnp.float32)  71 us
    all_to_all x1, blocking collectives, local(): lax.all_to_all(blocks, ('row', 'col'), split_axis=0, concat_axis=0, tiled...  38.8 us
    dot_general x16, matrix products, pair_step(): lax.dot_general(left_slab, right_slab, (((1,), (1,)), ((), ())), preferre...  38.7 us
    dynamic_slice x16, local copies, waits for them, and re-layouts, pair_step(): current = lax.dynamic_index_in_dim(gamma, own_slot, 0, keepdims=False)  29.2 us
  transfers between devices with their start and end apart: 1, of which 1 were waited for; matrix products, arithmetic and copies ran while one was open for 0% of the time, Pallas kernels for 0%

profile of v1, /device:TPU:1, one launch (start us, length us, event | category | flops | bytes accessed | tf_op | source)
XLA Modules:
  0.0 952.1 jit_solution(17124140610367806766)
XLA Ops:
  0.0 13.6 %stack.2 = bf16[16,2,384,1536]{3,2,1,0:T(8,128)(2,1)} broadcast(bf16[2,384,1536]{2,1,0:T(8,128)(2,1)} %param.8), dimensions={1,2,3} | broadcast | bytes 40108032 | tf_op jit(solution)/shard_map/stack | solution.py:9
  13.6 8.5 all-to-all-start
  22.1 564.2 %all-to-all-done = bf16[16,2,384,1536]{3,2,1,0:T(8,128)(2,1)} async-done(((bf16[16,2,384,1536]{3,2,1,0:T(8,128)(2,1)}), bf16[16,2,384,1536]{3,2,1,0:T(8,128)(2,1)}, u32[]{:S(2)}, u32[]{:S(2)}) %all-to-all-start) | async-done | bytes 37748768 | tf_op jit(solution)/shard_map/all_to_all | solution.py:10
  589.0 297.4 %while.15 = (s32[]{:T(128)}, f32[2,384,1536]{2,1,0:T(8,128)}, s32[1,16,2]{1,2,0:T(2,128)S(1)}, s32[1,16]{1,0:T(1,128)S(1)}, bf16[2,384,1536]{2,1,0:T(8,128)(2,1)...) while((s32[]{:T(128)}, f32[2,384,1536]{2,1,0:T(8,128)}, ...), condition=%wide.region_1.2_spmd, body=%wide.region_0.1_spmd.sunk | while | flops 908181888 | bytes 15937601 | solution.py:51
  603.2 4.4 fusion.40
  621.8 4.4 fusion.40
  640.4 4.4 fusion.40
  658.9 4.4 fusion.40
  677.5 4.4 fusion.40
  696.1 4.4 fusion.40
  714.7 4.4 fusion.40
  733.3 4.4 fusion.40
  751.9 4.4 fusion.40
  770.5 4.4 fusion.40
  789.0 4.4 fusion.40
  807.6 4.4 fusion.40
  826.2 4.4 fusion.40
  844.8 4.4 fusion.40
  863.4 4.4 fusion.40
  882.0 4.4 fusion.40
  890.4 4.9 reshape.28
  897.8 5.1 reshape.29
  905.4 38.8 %all_to_all.10 = bf16[128,2,4608]{2,1,0:T(2,128)(2,1)} all-to-all(bf16[128,2,4608]{2,1,0:T(2,128)(2,1)S(1)} %copy.15), channel_id=1, replica_groups=mesh['row'=8,'col'=16] {'row','col'}, dimensions={0} | all-to-all | bytes 4718592 | tf_op jit(solution)/shard_map/all_to_all | solution.py:62
  947.1 5.0 convolution_convert_fusion
  (127 shorter events, 128.0 us)
Async XLA Ops:
  0.0 947.1 %copy-start = (bf16[768,256]{1,0:T(8,128)(2,1)S(1)}, bf16[768,256]{1,0:T(8,128)(2,1)}, u32[]{:S(2)}) copy-start(bf16[768,256]{1,0:T(8,128)(2,1)} %param.11) | copy-start | bytes 1179652
  13.6 572.6 %all-to-all-start = ((bf16[16,2,384,1536]{3,2,1,0:T(8,128)(2,1)}), bf16[16,2,384,1536]{3,2,1,0:T(8,128)(2,1)}, u32[]{:S(2)}, u32[]{:S(2)}) async-start(bf16[16,2,384,1536]{3,2,1,0:T(8,128)(2,1)} %stack.2), calls=%async_computation | async-start | bytes 75497472 | tf_op jit(solution)/shard_map/all_to_all | solution.py:10
  586.2 2.8 copy-start.1
  586.2 2.8 copy-start.2
  586.2 2.8 copy-start.3
  586.2 2.8 copy-start.4
